TPU v7x, 256 devices: a whole 4x4x8 slice. The times are simulated.
256 devices in a mesh: row: 8 (over x_hi, y), col: 32 (over x_lo, z, core).
Axes of the slice: x: 4 (x_hi: 2, x_lo: 2; x = x_hi * 2 + x_lo), y: 4, z: 8, core: 2. Of those that a mesh axis runs over, the one named last changes fastest.
Arguments:
- forward_op: bfloat16 [12288, 98304], P('row', 'col'), may hold values from -0.01953125 to 0.01953125
- samples: bfloat16 [98304, 256], P('col'), may hold values from -6 to 6
- observed: float32 [256, 12288], P(None, 'row'), may hold values from -9 to 9
- precision: float32 [12288], P('row'), may hold values from 0.3 to 3
Outputs:
- adjoint: float32 [256, 98304], P('row', 'col')
All inputs are finite; a program needn't handle non-finite values.
Results may differ from a plain program's by a relative error of at most 0.0028.
Values may be sent and summed in bfloat16 or wider, within the bound.
A program may use at most 64 MiB of HBM per device.

v0:
```python
import jax
import jax.numpy as jnp
from jax import lax
from jax.sharding import PartitionSpec as P

dof = 4.0


def student_score(error, precision):
    return (dof + 1.0) * precision * error / (dof + precision * error * error)


def local(forward_op, samples, observed, precision):
    weights = precision[None, :]
    share = observed.shape[0] // lax.axis_size("col")
    block = samples
    predicted = lax.psum_scatter(
        lax.dot_general(
            block, forward_op, (((0,), (1,)), ((), ())), preferred_element_type=jnp.float32
        ),
        "col",
        scatter_dimension=0,
        tiled=True,
    )
    mine = lax.dynamic_slice_in_dim(observed, lax.axis_index("col") * share, share, 0)
    own_scores = student_score(mine - predicted, weights).astype(jnp.bfloat16)
    scores = lax.all_gather(own_scores, "col", axis=0, tiled=True)
    block = scores
    return lax.psum_scatter(
        jnp.dot(block, forward_op, preferred_element_type=jnp.float32),
        "row",
        scatter_dimension=0,
        tiled=True,
    )


def solution(mesh):
    return jax.shard_map(
        local,
        mesh=mesh,
        in_specs=(P("row", "col"), P("col", None), P(None, "row"), P("row")),
        out_specs=P("row", "col"),
        check_vma=False,
    )
```

profile of v0, /device:TPU:1, one launch (start us, length us, event | category | flops | bytes accessed | tf_op | source)
XLA Modules:
  0.0 265.4 jit_solution(6132793075065170543)
XLA Ops:
  6.5 0.0 copy-start
  6.5 0.0 copy-start.1
  6.5 0.0 reduce-scatter.3.cloned.1.call-start
  6.5 1.4 copy-done
  7.9 7.5 %fusion.3 = f32[256,1536]{1,0:T(8,128)} fusion(bf16[3072,256]{1,0:T(8,128)(2,1)S(1)} %copy-done, bf16[1536,3072]{1,0:T(8,128)(2,1)} %param.4), kind=kOutput, calls=%fused_computation.5 | convolution fusion | flops 2415919104 | bytes 12582912 | tf_op jit(solution)/shard_map/dot_general | solution.py:18
  15.5 0.0 reduce-scatter.3.cloned.1.call-update
  15.5 0.0 reduce-scatter.5.cloned.1.call-start
  15.5 0.0 copy-done.1
  15.6 117.7 %reduce-scatter.3.cloned.1.call-done = f32[8,1536]{1,0:T(8,128)} async-done(((f32[256,1536]{1,0:T(8,128)}), f32[8,1536]{1,0:T(8,128)}) %reduce-scatter.3.cloned.1.call-update) | async-done | bytes 49168 | tf_op jit(solution)/shard_map/reduce_scatter | solution.py:17
  133.3 0.8 fusion.2
  134.1 36.9 %all_gather.3 = bf16[256,1536]{1,0:T(8,128)(2,1)S(1)} all-gather(bf16[8,1536]{1,0:T(8,128)(2,1)S(1)} %fusion.2), channel_id=1, replica_groups=mesh['row'=8,'col'=32] {'col'}, dimensions={0}, use_global_device_ids=true | all-gather | bytes 811008 | tf_op jit(solution)/shard_map/all_gather | solution.py:27
  171.0 7.9 %fusion.4 = f32[256,3072]{1,0:T(8,128)} fusion(bf16[256,1536]{1,0:T(8,128)(2,1)S(1)} %all_gather.3, bf16[1536,3072]{1,0:T(8,128)(2,1)} %param.4), kind=kOutput, calls=%fused_computation.6 | convolution fusion | flops 2415919104 | bytes 13369344 | tf_op jit(solution)/shard_map/dot_general | solution.py:30
  178.9 0.0 reduce-scatter.5.cloned.1.call-update
  179.0 79.6 %reduce-scatter.5.cloned.1.call-done = f32[32,3072]{1,0:T(8,128)} async-done(((f32[256,3072]{1,0:T(8,128)}), f32[32,3072]{1,0:T(8,128)}) %reduce-scatter.5.cloned.1.call-update) | async-done | bytes 393232 | tf_op jit(solution)/shard_map/reduce_scatter | solution.py:29
  (1 shorter events, 0.0 us)
Async XLA Ops:
  6.5 1.4 copy-start
  6.5 9.0 %copy-start.1 = (f32[1536]{0:T(1024)S(1)}, f32[1536]{0:T(1024)}, u32[]{:S(2)}) copy-start(f32[1536]{0:T(1024)} %param.7) | copy-start | bytes 18436
  6.5 126.8 %reduce-scatter.3.cloned.1.call-start = ((), (), s32[]{:S(2)}) async-start(), calls=%async_computation.2 | async-start | bytes 1622016 | tf_op jit(solution)/shard_map/reduce_scatter | solution.py:17
  15.5 243.1 %reduce-scatter.5.cloned.1.call-start = ((), (), s32[]{:S(2)}) async-start(), calls=%async_computation.3 | async-start | bytes 3538944 | tf_op jit(solution)/shard_map/reduce_scatter | solution.py:29
Sparse Core Ops, SparseCore 0:
  15.6 117.6 reduce-scatter.2
  179.1 79.4 reduce-scatter.4
where the time goes:
time: 266 us; the launch traced here: 265 us
  waiting for transfers between devices  197 us (74%)
  blocking collectives  36.9 us (14%)
  matrix products  15.4 us (6%)
  between operations  13.4 us (5%)
    reduce_scatter x1, waiting for transfers between devices, local(): lax.psum_scatter(lax.dot_general(block, forward_op, (((0,), (1,)), ((), (...  118 us
    reduce_scatter x1, waiting for transfers between devices, local(): lax.psum_scatter(jnp.dot(block, forward_op, preferred_element_type=jnp.fl...  79.6 us
    all_gather x1, blocking collectives, local(): scores = lax.all_gather(own_scores, 'col', axis=0, tiled=True)  36.9 us
    dot_general x1, matrix products, local(): jnp.dot(block, forward_op, preferred_element_type=jnp.float32)  7.93 us
    dot_general x1, matrix products, local(): lax.dot_general(block, forward_op, (((0,), (1,)), ((), ())), preferred_el...  7.51 us
  transfers between devices with their start and end apart: 2, of which 2 were waited for; matrix products, arithmetic and copies ran while one was open for 0% of the time, Pallas kernels for 0%

commit v1 on v0

v1 whole, which is shorter than its diff:
```python
import jax
import jax.numpy as jnp
from jax import lax
from jax.experimental import pallas as pl
from jax.experimental.pallas import tpu as pltpu
from jax.sharding import PartitionSpec as P

MESH = pl.DeviceIdType.MESH
F32 = jnp.float32
BF16 = jnp.bfloat16

S = 256
MB = 1536
NB = 3072
UNIT = 48
BLK = 384
NC = 256
PAIRS = NB // NC // 2
LAG = 1
TINY = 1e-36
FAR = (4, 3, 5, 2, 6, 1, 7)
NEAR = (1, 7, 2, 6, 3, 5, 4)
dof = 4.0


def enc4(v):
    w = v * v
    return (v * jnp.abs(v) * w).astype(BF16)


def dec4(c):
    v = c.astype(F32)
    t = lax.rsqrt(jnp.maximum(jnp.abs(v), TINY))
    return v * (t * t * lax.rsqrt(t))


def enc2(v):
    return (v * jnp.abs(v)).astype(BF16)


def dec2(c):
    v = c.astype(F32)
    return v * lax.rsqrt(jnp.maximum(jnp.abs(v), TINY))


def student_score(error, precision):
    return (dof + 1.0) * precision * error / (dof + precision * error * error)


def kernel(
    fop_hbm, samp_hbm, obs_hbm, prec_ref, out_ref,
    fop, samp, obs, obs_t, prec_t,
    sib_send, sib_recv, acc, quad, own, x_send, x_recv, z_send, z_recv,
    sc_t, sc, parts, r_send, r_recv, held, h_send, h_recv,
    load_sem, sib_sem, x_sem, z_sem, gz_sem, gx_sem, gs_sem, r_sem, h_sem,
):
    row = lax.axis_index("row")
    col = lax.axis_index("col")
    xh, y = row // 4, row % 4
    xl, z, core = col // 16, (col // 2) % 8, col % 2

    def at_col(x_, z_, c_):
        return (row, x_ * 16 + z_ * 2 + c_)

    sibling = at_col(xl, z, 1 - core)
    xpart = at_col(1 - xl, z, core)
    hpart = ((1 - xh) * 4 + y, col)

    def zpeer(d):
        return at_col(xl, (z + d) % 8, core)

    def ypeer(g):
        return (xh * 4 + (y + g) % 4, col)

    def block_at(c_, x_):
        return pl.multiple_of((c_ * 2 + x_) * BLK, BLK)

    order = ((1 - core, 1 - xl), (1 - core, xl), (core, 1 - xl), (core, xl))
    mine = block_at(core, xl)

    load_samp = pltpu.make_async_copy(samp_hbm, samp, load_sem.at[4])
    load_samp.start()
    load_fop = []
    for j, (c_, x_) in enumerate(order):
        rows = pl.ds(block_at(c_, x_), BLK)
        cp = pltpu.make_async_copy(fop_hbm.at[rows], fop.at[rows], load_sem.at[j])
        cp.start()
        load_fop.append(cp)
    load_obs = pltpu.make_async_copy(obs_hbm.at[:, pl.ds(mine, BLK)], obs, load_sem.at[5])
    load_obs.start()

    barrier = pltpu.get_barrier_semaphore()
    peers = [sibling, xpart, hpart, ypeer(1), ypeer(3)] + [zpeer(d) for d in range(1, 8)]
    for p in peers:
        pl.semaphore_signal(barrier, inc=1, device_id=p, device_id_type=MESH)
    pl.semaphore_wait(barrier, len(peers))

    def remote(src, dst, sems, i, device):
        return pltpu.make_async_remote_copy(
            src_ref=src, dst_ref=dst, send_sem=sems.at[(0,) + i], recv_sem=sems.at[(1,) + i],
            device_id=device, device_id_type=MESH,
        )

    sends = []

    def go(cp):
        cp.start()
        sends.append(cp)
        return cp

    def product(j):
        load_fop[j].wait()
        rows = pl.ds(block_at(*order[j]), BLK)
        return jnp.dot(fop[rows, :], samp[...], preferred_element_type=F32)

    load_samp.wait()
    sib = []
    for j in range(2):
        sib_send[j] = product(j)
        sib.append(go(remote(sib_send.at[j], sib_recv.at[j], sib_sem, (j,), sibling)))
    acc[...] = product(2)
    sib[0].wait_recv()
    xs = {}
    for d in FAR + (0,):
        rows = pl.ds(pl.multiple_of(((z + d) % 8) * UNIT, UNIT), UNIT)
        x_send[d] = enc4(acc[rows, :] + sib_recv[0, rows, :])
        xs[d] = go(remote(x_send.at[d], x_recv.at[d], x_sem, (d,), xpart))
    quad[...] = product(3)
    sib[1].wait_recv()
    zs = {}
    for d in FAR + (0,):
        rows = pl.ds(pl.multiple_of(((z + d) % 8) * UNIT, UNIT), UNIT)
        xs[d].wait_recv()
        v = quad[rows, :] + sib_recv[1, rows, :] + dec4(x_recv[d])
        if d:
            z_send[d] = enc4(v)
            zs[d] = go(remote(z_send.at[d], z_recv.at[d], z_sem, (d,), zpeer(d)))
        else:
            own[...] = v

    load_obs.wait()
    obs_t[...] = obs[...].T
    prec_t[...] = jnp.broadcast_to(prec_ref[:, pl.ds(mine, BLK)], (128, BLK)).T

    pred = own[...]
    for d in NEAR:
        zs[d].wait_recv()
        pred = pred + dec4(z_recv[d])
    rows = pl.ds(pl.multiple_of(z * UNIT, UNIT), UNIT)
    p = prec_t[rows, :]
    p = jnp.concatenate([p, p], axis=1)
    score = student_score(obs_t[rows, :] - pred, p).astype(BF16)

    def unit_at(x_, z_):
        return sc_t.at[pl.ds(pl.multiple_of((core * 2 + x_) * BLK + z_ * UNIT, 16), UNIT)]

    unit_at(xl, z)[...] = score

    def to_x(d):
        zz = (z + 8 - d) % 8
        return remote(unit_at(xl, zz), unit_at(xl, zz), gx_sem, (d,), xpart)

    gx = {0: go(to_x(0))}
    gz = {}
    for d in FAR:
        gz[d] = go(remote(unit_at(xl, z), unit_at(xl, z), gz_sem, (d,), zpeer(d)))
    for d in NEAR:
        gz[d].wait_recv()
        gx[d] = go(to_x(d))

    def to_sibling(k):
        b = sc_t.at[pl.ds(block_at(*order[2 + k]), BLK)]
        return remote(b, b, gs_sem, (k,), sibling)

    def turn(j):
        b = pl.ds(block_at(*order[j]), BLK)
        sc[:, b] = sc_t[b, :].T

    g1 = go(to_sibling(1))
    turn(3)
    for d in (0,) + NEAR:
        gx[d].wait_recv()
    g0 = go(to_sibling(0))
    turn(2)
    g1.wait_recv()
    turn(1)
    g0.wait_recv()
    turn(0)

    def ring(c, s, g):
        return remote(r_send.at[c, s], r_recv.at[c, s], r_sem, (c, s), ypeer(g))

    def far(c):
        return remote(h_send.at[c], h_recv.at[c], h_sem, (c,), hpart)

    def block(c, b):
        lo = parts[c, pl.ds(pl.multiple_of(b * 32, 32), 32), :]
        hi = parts[c, pl.ds(pl.multiple_of(128 + b * 32, 32), 32), :]
        return jnp.concatenate([lo, hi], axis=0)

    def step(t, carry):
        for way, g in enumerate((1, 3)):
            @pl.when(t < PAIRS)
            def _():
                c = 2 * t + way
                columns = pl.ds(pl.multiple_of(c * NC, NC), NC)
                parts[c] = jnp.dot(sc[...], fop[:, columns], preferred_element_type=F32)
                r_send[c, 0] = enc2(block(c, (y + 4 - g) % 4))
                ring(c, 0, g).start()

        for s in (1, 2, 3):
            u = t - s * LAG

            @pl.when((u >= 0) & (u < PAIRS))
            def _():
                for way, g in enumerate((1, 3)):
                    c = 2 * u + way
                    ring(c, s - 1, g).wait_recv()
                    v = dec2(r_recv[c, s - 1]) + block(c, (y + (4 - g) * (s + 1)) % 4)
                    if s < 3:
                        r_send[c, s] = enc2(v)
                        ring(c, s, g).start()
                    else:
                        held[c] = v
                        h_send[c] = enc2(held[c, pl.ds(pl.multiple_of((1 - xh) * 32, 32), 32), :])
                        far(c).start()

        w = t - 4 * LAG

        @pl.when((w >= 0) & (w < PAIRS))
        def _():
            for way in range(2):
                c = 2 * w + way
                columns = pl.ds(pl.multiple_of(c * NC, NC), NC)
                far(c).wait_recv()
                out_ref[:, columns] = held[c, pl.ds(pl.multiple_of(xh * 32, 32), 32), :] + dec2(h_recv[c])

        return carry

    lax.fori_loop(0, PAIRS + 4 * LAG, step, 0)

    for cp in sends:
        cp.wait_send()

    def drain(t, carry):
        for way, g in enumerate((1, 3)):
            c = 2 * t + way
            for s in range(3):
                ring(c, s, g).wait_send()
            far(c).wait_send()
        return carry

    lax.fori_loop(0, PAIRS, drain, 0)


def local(forward_op, samples, observed, precision):
    chunks = NB // NC
    dma = pltpu.SemaphoreType.DMA
    return pl.pallas_call(
        kernel,
        out_shape=jax.ShapeDtypeStruct((S // 8, NB), F32),
        in_specs=[pl.BlockSpec(memory_space=pltpu.HBM)] * 3 + [pl.BlockSpec(memory_space=pltpu.VMEM)],
        out_specs=pl.BlockSpec(memory_space=pltpu.VMEM),
        scratch_shapes=[
            pltpu.VMEM((MB, NB), BF16),
            pltpu.VMEM((NB, S), BF16),
            pltpu.VMEM((S, BLK), F32),
            pltpu.VMEM((BLK, S), F32),
            pltpu.VMEM((BLK, 128), F32),
            pltpu.VMEM((2, BLK, S), F32),
            pltpu.VMEM((2, BLK, S), F32),
            pltpu.VMEM((BLK, S), F32),
            pltpu.VMEM((BLK, S), F32),
            pltpu.VMEM((UNIT, S), F32),
            pltpu.VMEM((8, UNIT, S), BF16),
            pltpu.VMEM((8, UNIT, S), BF16),
            pltpu.VMEM((8, UNIT, S), BF16),
            pltpu.VMEM((8, UNIT, S), BF16),
            pltpu.VMEM((MB, S), BF16),
            pltpu.VMEM((S, MB), BF16),
            pltpu.VMEM((chunks, S, NC), F32),
            pltpu.VMEM((chunks, 3, 64, NC), BF16),
            pltpu.VMEM((chunks, 3, 64, NC), BF16),
            pltpu.VMEM((chunks, 64, NC), F32),
            pltpu.VMEM((chunks, 32, NC), BF16),
            pltpu.VMEM((chunks, 32, NC), BF16),
            dma((6,)),
            dma((2, 2)),
            dma((2, 8)),
            dma((2, 8)),
            dma((2, 8)),
            dma((2, 8)),
            dma((2, 2)),
            dma((2, chunks, 3)),
            dma((2, chunks)),
        ],
        compiler_params=pltpu.CompilerParams(
            collective_id=0, has_side_effects=True, vmem_limit_bytes=48 * 1024 * 1024
        ),
    )(forward_op, samples, observed, precision.reshape(1, MB))


def solution(mesh):
    return jax.shard_map(
        local,
        mesh=mesh,
        in_specs=(P("row", "col"), P("col", None), P(None, "row"), P("row")),
        out_specs=P("row", "col"),
        check_vma=False,
    )
```

time: 266 us -> 66.7 us (0.25)
  the two profiles are of different devices: /device:TPU:1 before, /device:TPU:4 now
where the time goes in v1:
time: 66.7 us; the launch traced here: 66.5 us
  Pallas kernels  62.2 us (93%)
  local copies, waits for them, and re-layouts  4.26 us (6%)
    pallas_call x1, Pallas kernels, local(): pl.pallas_call(kernel, out_shape=jax.ShapeDtypeStruct((S // 8, NB), F32),...  62.2 us
    unnamed x5, local copies, waits for them, and re-layouts  3.56 us

profile of v1, /device:TPU:4, one launch (start us, length us, event | category | flops | bytes accessed | tf_op | source)
XLA Modules:
  0.0 66.5 jit_solution(15355162131926262722)
XLA Ops:
  0.0 0.7 %reshape.3.prec_ref = f32[1,1536]{1,0:T(1,128)S(1)} reshape(f32[1536]{0:T(1024)} %param.7) | data formatting | bytes 12288 | tf_op jit(solution)/shard_map/reshape | solution.py:300
  0.7 0.0 copy-start
  0.7 1.4 %copy-done = bf16[3072,256]{1,0:T(8,128)(2,1)S(1)} copy-done((bf16[3072,256]{1,0:T(8,128)(2,1)S(1)}, bf16[3072,256]{1,0:T(8,128)(2,1)}, u32[]{:S(2)}) %copy-start) | copy-done | bytes 1572888
  2.1 0.0 copy-start.1
  2.1 1.4 %copy-done.1 = f32[256,1536]{1,0:T(8,128)S(1)} copy-done((f32[256,1536]{1,0:T(8,128)S(1)}, f32[256,1536]{1,0:T(8,128)}, u32[]{:S(2)}) %copy-start.1) | copy-done | bytes 1572888
  3.5 62.2 %shard_map.46 = f32[32,3072]{1,0:T(8,128)S(1)} custom-call(bf16[1536,3072]{1,0:T(8,128)(2,1)} %fop_hbm.1, bf16[3072,256]{1,0:T(8,128)(2,1)S(1)} %copy-done, f32[256,1536]{1,0:T(8,128)S(1)} %copy-done.1, f32[1,1536]{1,0:T(1,128)S(1)} %reshape.3.prec_ref), custom_call_target="tpu_custom_call" | custom-call | tf_op jit(solution)/shard_map/pallas_call | solution.py:259
  65.7 0.7 %copy.6 = f32[32,3072]{1,0:T(8,128)} copy(f32[32,3072]{1,0:T(8,128)S(1)} %shard_map.46) | data formatting | bytes 786432
Async XLA Ops:
  0.7 1.4 %copy-start = (bf16[3072,256]{1,0:T(8,128)(2,1)S(1)}, bf16[3072,256]{1,0:T(8,128)(2,1)}, u32[]{:S(2)}) copy-start(bf16[3072,256]{1,0:T(8,128)(2,1)} %samp_hbm.1) | copy-start | bytes 4718596
  2.1 1.4 %copy-start.1 = (f32[256,1536]{1,0:T(8,128)S(1)}, f32[256,1536]{1,0:T(8,128)}, u32[]{:S(2)}) copy-start(f32[256,1536]{1,0:T(8,128)} %obs_hbm.1) | copy-start | bytes 4718596

commit v2 on v1

v2 whole, which is shorter than its diff:
```python
import jax
import jax.numpy as jnp
from jax import lax
from jax.experimental import pallas as pl
from jax.experimental.pallas import tpu as pltpu
from jax.sharding import PartitionSpec as P

MESH = pl.DeviceIdType.MESH
F32 = jnp.float32
BF16 = jnp.bfloat16

S = 256
MB = 1536
NB = 3072
UNIT = 48
BLK = 384
NC = 256
CHUNKS = NB // NC
YF = 5
XF = CHUNKS - YF
TINY = 1e-36
FAR = (4, 3, 5, 2, 6, 1, 7)
NEAR = (1, 7, 2, 6, 3, 5, 4)
dof = 4.0


def enc4(v):
    w = v * v
    return (v * jnp.abs(v) * w).astype(BF16)


def dec4(c):
    v = c.astype(F32)
    t = lax.rsqrt(jnp.maximum(jnp.abs(v), TINY))
    return v * (t * t * lax.rsqrt(t))


def enc2(v):
    return (v * jnp.abs(v)).astype(BF16)


def dec2(c):
    v = c.astype(F32)
    return v * lax.rsqrt(jnp.maximum(jnp.abs(v), TINY))


def student_score(error, precision):
    return (dof + 1.0) * precision * error / (dof + precision * error * error)


def kernel(
    fop_hbm, samp_hbm, obs_hbm, prec_hbm, out_ref,
    fop, samp, obs, prec, obs_t, prec_t,
    sib_send, sib_recv, acc, quad, own, x_send, x_recv, z_send, z_recv,
    sc_t, sc, parts, held, xx_send, xx_recv, xy_send, xy_recv, yy_send, yy_recv, yx_send, yx_recv,
    load_sem, sib_sem, x_sem, z_sem, gz_sem, gx_sem, gs_sem, xx_sem, xy_sem, yy_sem, yx_sem,
):
    row = lax.axis_index("row")
    col = lax.axis_index("col")
    xh, y = row // 4, row % 4
    xl, z, core = col // 16, (col // 2) % 8, col % 2

    def at_col(x_, z_, c_):
        return (row, x_ * 16 + z_ * 2 + c_)

    sibling = at_col(xl, z, 1 - core)
    xpart = at_col(1 - xl, z, core)
    hpart = ((1 - xh) * 4 + y, col)

    def zpeer(d):
        return at_col(xl, (z + d) % 8, core)

    def ypeer(d):
        return (xh * 4 + (y + d) % 4, col)

    def block_at(c_, x_):
        return pl.multiple_of((c_ * 2 + x_) * BLK, BLK)

    order = ((1 - core, 1 - xl), (core, 1 - xl), (1 - core, xl), (core, xl))
    mine = block_at(core, xl)

    load_samp = pltpu.make_async_copy(samp_hbm, samp, load_sem.at[4])
    load_samp.start()
    load_fop = []
    for j, (c_, x_) in enumerate(order):
        rows = pl.ds(block_at(c_, x_), BLK)
        cp = pltpu.make_async_copy(fop_hbm.at[rows], fop.at[rows], load_sem.at[j])
        cp.start()
        load_fop.append(cp)
    load_obs = pltpu.make_async_copy(obs_hbm.at[:, pl.ds(mine, BLK)], obs, load_sem.at[5])
    load_obs.start()
    load_prec = pltpu.make_async_copy(prec_hbm, prec, load_sem.at[6])
    load_prec.start()

    barrier = pltpu.get_barrier_semaphore()
    peers = [sibling, xpart, hpart, ypeer(1), ypeer(2), ypeer(3)] + [zpeer(d) for d in range(1, 8)]
    for p in peers:
        pl.semaphore_signal(barrier, inc=1, device_id=p, device_id_type=MESH)
    pl.semaphore_wait(barrier, len(peers))

    def remote(src, dst, sems, i, device):
        return pltpu.make_async_remote_copy(
            src_ref=src, dst_ref=dst, send_sem=sems.at[(0,) + i], recv_sem=sems.at[(1,) + i],
            device_id=device, device_id_type=MESH,
        )

    sends = []

    def go(cp):
        cp.start()
        sends.append(cp)
        return cp

    def product(j):
        load_fop[j].wait()
        rows = pl.ds(block_at(*order[j]), BLK)
        return jnp.dot(fop[rows, :], samp[...], preferred_element_type=F32)

    load_samp.wait()
    sib_send[0] = product(0)
    sib0 = go(remote(sib_send.at[0], sib_recv.at[0], sib_sem, (0,), sibling))
    acc[...] = product(1)
    sib0.wait_recv()
    xs = {}
    for d in FAR + (0,):
        rows = pl.ds(pl.multiple_of(((z + d) % 8) * UNIT, UNIT), UNIT)
        x_send[d] = enc4(acc[rows, :] + sib_recv[0, rows, :])
        xs[d] = go(remote(x_send.at[d], x_recv.at[d], x_sem, (d,), xpart))
    sib_send[1] = product(2)
    sib1 = go(remote(sib_send.at[1], sib_recv.at[1], sib_sem, (1,), sibling))
    quad[...] = product(3)
    sib1.wait_recv()
    zs = {}
    for d in FAR + (0,):
        rows = pl.ds(pl.multiple_of(((z + d) % 8) * UNIT, UNIT), UNIT)
        xs[d].wait_recv()
        v = quad[rows, :] + sib_recv[1, rows, :] + dec4(x_recv[d])
        if d:
            z_send[d] = enc4(v)
            zs[d] = go(remote(z_send.at[d], z_recv.at[d], z_sem, (d,), zpeer(d)))
        else:
            own[...] = v

    load_obs.wait()
    load_prec.wait()
    obs_t[...] = obs[...].T
    prec_t[...] = jnp.broadcast_to(prec[pl.ds(mine, BLK)].reshape(1, BLK), (128, BLK)).T

    pred = own[...]
    for d in NEAR:
        zs[d].wait_recv()
        pred = pred + dec4(z_recv[d])
    rows = pl.ds(pl.multiple_of(z * UNIT, UNIT), UNIT)
    p = prec_t[rows, :]
    p = jnp.concatenate([p, p], axis=1)
    score = student_score(obs_t[rows, :] - pred, p).astype(BF16)

    def unit_at(x_, z_):
        return sc_t.at[pl.ds(pl.multiple_of((core * 2 + x_) * BLK + z_ * UNIT, 16), UNIT)]

    unit_at(xl, z)[...] = score

    def to_x(d):
        zz = (z + 8 - d) % 8
        return remote(unit_at(xl, zz), unit_at(xl, zz), gx_sem, (d,), xpart)

    gx = {0: go(to_x(0))}
    gz = {}
    for d in NEAR:
        gz[d] = go(remote(unit_at(xl, z), unit_at(xl, z), gz_sem, (d,), zpeer(d)))
    for d in NEAR:
        gz[d].wait_recv()
        gx[d] = go(to_x(d))

    def to_sibling(k):
        b = sc_t.at[pl.ds(block_at(core, (1 - xl, xl)[k]), BLK)]
        return remote(b, b, gs_sem, (k,), sibling)

    def turn(j):
        b = pl.ds(block_at(*order[j]), BLK)
        sc[:, b] = sc_t[b, :].T

    g1 = go(to_sibling(1))
    turn(3)
    for d in (0,) + NEAR:
        gx[d].wait_recv()
    g0 = go(to_sibling(0))
    turn(1)
    g1.wait_recv()
    turn(2)
    g0.wait_recv()
    turn(0)

    def columns(c):
        return pl.ds(pl.multiple_of(c * NC, NC), NC)

    def dest(x_, y_):
        return pl.ds(pl.multiple_of(x_ * 128 + y_ * 32, 32), 32)

    def half(x_):
        return pl.ds(pl.multiple_of(x_ * 128, 128), 128)

    def xx(i):
        return remote(xx_send.at[i], xx_recv.at[i], xx_sem, (i,), hpart)

    def xy(i, d):
        return remote(xy_send.at[i, d - 1], xy_recv.at[i, d - 1], xy_sem, (i, d - 1), ypeer(d))

    def yy(j, d):
        return remote(yy_send.at[j, d - 1], yy_recv.at[j, d - 1], yy_sem, (j, d - 1), ypeer(d))

    def yx(j):
        return remote(yx_send.at[j], yx_recv.at[j], yx_sem, (j,), hpart)

    def adjoint(c):
        parts[c] = jnp.dot(sc[...], fop[:, columns(c)], preferred_element_type=F32)

    def x_first(i, c):
        adjoint(c)
        xx_send[i] = enc2(parts[c, half(1 - xh), :])
        xx(i).start()

    def y_first(j, c):
        adjoint(c)
        for d in (2, 1, 3):
            y_ = (y + d) % 4
            yy_send[j, d - 1, :32] = enc2(parts[c, dest(0, y_), :])
            yy_send[j, d - 1, 32:] = enc2(parts[c, dest(1, y_), :])
            yy(j, d).start()

    def x_then_y(i, c):
        xx(i).wait_recv()
        for d in (2, 1, 3, 0):
            y_ = (y + d) % 4
            v = parts[c, dest(xh, y_), :] + dec2(xx_recv[i, pl.ds(pl.multiple_of(y_ * 32, 32), 32), :])
            if d:
                xy_send[i, d - 1] = enc2(v)
                xy(i, d).start()
            else:
                held[c] = v

    def y_then_x(j, c):
        for d in (1, 3, 2):
            yy(j, d).wait_recv()

        def total(x_):
            v = parts[c, dest(x_, y), :]
            for d in (1, 2, 3):
                v = v + dec2(yy_recv[j, d - 1, pl.ds(pl.multiple_of(x_ * 32, 32), 32), :])
            return v

        yx_send[j] = enc2(total(1 - xh))
        yx(j).start()
        held[c] = total(xh)

    def end_x_first(i, c):
        v = held[c]
        for d in (1, 3, 2):
            xy(i, d).wait_recv()
            v = v + dec2(xy_recv[i, d - 1])
        out_ref[:, columns(c)] = v

    def end_y_first(j, c):
        yx(j).wait_recv()
        out_ref[:, columns(c)] = held[c] + dec2(yx_recv[j])

    def drain_x(i, c):
        xx(i).wait_send()
        for d in (1, 2, 3):
            xy(i, d).wait_send()

    def drain_y(j, c):
        yx(j).wait_send()
        for d in (1, 2, 3):
            yy(j, d).wait_send()

    def sweep(on_x, on_y):
        def both(t, carry):
            on_x(t, 2 * t)
            on_y(t, 2 * t + 1)
            return carry

        def rest(t, carry):
            on_x(t, t + YF)
            return carry

        lax.fori_loop(0, YF, both, 0)
        lax.fori_loop(YF, XF, rest, 0)

    sweep(x_first, y_first)
    sweep(x_then_y, y_then_x)
    sweep(end_x_first, end_y_first)
    for cp in sends:
        cp.wait_send()
    sweep(drain_x, drain_y)


def local(forward_op, samples, observed, precision):
    dma = pltpu.SemaphoreType.DMA
    return pl.pallas_call(
        kernel,
        out_shape=jax.ShapeDtypeStruct((S // 8, NB), F32),
        in_specs=[pl.BlockSpec(memory_space=pltpu.HBM)] * 4,
        out_specs=pl.BlockSpec(memory_space=pltpu.VMEM),
        scratch_shapes=[
            pltpu.VMEM((MB, NB), BF16),
            pltpu.VMEM((NB, S), BF16),
            pltpu.VMEM((S, BLK), F32),
            pltpu.VMEM((MB,), F32),
            pltpu.VMEM((BLK, S), F32),
            pltpu.VMEM((BLK, 128), F32),
            pltpu.VMEM((2, BLK, S), F32),
            pltpu.VMEM((2, BLK, S), F32),
            pltpu.VMEM((BLK, S), F32),
            pltpu.VMEM((BLK, S), F32),
            pltpu.VMEM((UNIT, S), F32),
            pltpu.VMEM((8, UNIT, S), BF16),
            pltpu.VMEM((8, UNIT, S), BF16),
            pltpu.VMEM((8, UNIT, S), BF16),
            pltpu.VMEM((8, UNIT, S), BF16),
            pltpu.VMEM((MB, S), BF16),
            pltpu.VMEM((S, MB), BF16),
            pltpu.VMEM((CHUNKS, S, NC), F32),
            pltpu.VMEM((CHUNKS, 32, NC), F32),
            pltpu.VMEM((XF, 128, NC), BF16),
            pltpu.VMEM((XF, 128, NC), BF16),
            pltpu.VMEM((XF, 3, 32, NC), BF16),
            pltpu.VMEM((XF, 3, 32, NC), BF16),
            pltpu.VMEM((YF, 3, 64, NC), BF16),
            pltpu.VMEM((YF, 3, 64, NC), BF16),
            pltpu.VMEM((YF, 32, NC), BF16),
            pltpu.VMEM((YF, 32, NC), BF16),
            dma((7,)),
            dma((2, 2)),
            dma((2, 8)),
            dma((2, 8)),
            dma((2, 8)),
            dma((2, 8)),
            dma((2, 2)),
            dma((2, XF)),
            dma((2, XF, 3)),
            dma((2, YF, 3)),
            dma((2, YF)),
        ],
        compiler_params=pltpu.CompilerParams(
            collective_id=0, has_side_effects=True, vmem_limit_bytes=48 * 1024 * 1024
        ),
    )(*[pltpu.with_memory_space_constraint(a, pltpu.HBM) for a in (forward_op, samples, observed, precision)])


def solution(mesh):
    return jax.shard_map(
        local,
        mesh=mesh,
        in_specs=(P("row", "col"), P("col", None), P(None, "row"), P("row")),
        out_specs=P("row", "col"),
        check_vma=False,
    )
```

time: 66.7 us -> 54.5 us (0.82)
  the two profiles are of different devices: /device:TPU:4 before, /device:TPU:1 now
where the time goes in v2:
time: 54.5 us; the launch traced here: 54.4 us
  Pallas kernels  53.6 us (98%)
  local copies, waits for them, and re-layouts  0.75 us (1%)
    pallas_call x1, Pallas kernels, local(): pl.pallas_call(kernel, out_shape=jax.ShapeDtypeStruct((S // 8, NB), F32),...  53.6 us

profile of v2, /device:TPU:1, one launch (start us, length us, event | category | flops | bytes accessed | tf_op | source)
XLA Modules:
  0.0 54.4 jit_solution(7619033460445542888)
XLA Ops:
  0.0 53.6 %shard_map.46 = f32[32,3072]{1,0:T(8,128)S(1)} custom-call(bf16[1536,3072]{1,0:T(8,128)(2,1)} %fop_hbm.1, bf16[3072,256]{1,0:T(8,128)(2,1)} %samp_hbm.1, f32[256,1536]{1,0:T(8,128)} %obs_hbm.1, f32[1536]{0:T(1024)} %prec_hbm.1), custom_call_target="tpu_custom_call" | custom-call | tf_op jit(solution)/shard_map/pallas_call | solution.py:300
  53.7 0.7 %copy.6 = f32[32,3072]{1,0:T(8,128)} copy(f32[32,3072]{1,0:T(8,128)S(1)} %shard_map.46) | data formatting | bytes 786432

commit v3 on v2

--- a/solution.py
+++ b/solution.py
@@ -16,11 +16,13 @@
 BLK = 384
 NC = 256
 CHUNKS = NB // NC
-YF = 5
+YF = 6
 XF = CHUNKS - YF
 TINY = 1e-36
 FAR = (4, 3, 5, 2, 6, 1, 7)
 NEAR = (1, 7, 2, 6, 3, 5, 4)
+RDIRECT = ()
+GDIRECT = (1, 7, 2, 6)
 dof = 4.0
 
 
@@ -51,9 +53,9 @@
 def kernel(
     fop_hbm, samp_hbm, obs_hbm, prec_hbm, out_ref,
     fop, samp, obs, prec, obs_t, prec_t,
-    sib_send, sib_recv, acc, quad, own, x_send, x_recv, z_send, z_recv,
+    sib_send, sib_recv, acc, quad, x_send, x_recv, z_send, z_recv, zx_recv,
     sc_t, sc, parts, held, xx_send, xx_recv, xy_send, xy_recv, yy_send, yy_recv, yx_send, yx_recv,
-    load_sem, sib_sem, x_sem, z_sem, gz_sem, gx_sem, gs_sem, xx_sem, xy_sem, yy_sem, yx_sem,
+    load_sem, sib_sem, x_sem, z_sem, zx_sem, gz_sem, gx_sem, gs_sem, xx_sem, xy_sem, yy_sem, yx_sem,
 ):
     row = lax.axis_index("row")
     col = lax.axis_index("col")
@@ -70,6 +72,9 @@
     def zpeer(d):
         return at_col(xl, (z + d) % 8, core)
 
+    def across(d):
+        return at_col(1 - xl, (z + d) % 8, core)
+
     def ypeer(d):
         return (xh * 4 + (y + d) % 4, col)
 
@@ -80,23 +85,20 @@
     mine = block_at(core, xl)
 
     load_samp = pltpu.make_async_copy(samp_hbm, samp, load_sem.at[4])
-    load_samp.start()
     load_fop = []
     for j, (c_, x_) in enumerate(order):
         rows = pl.ds(block_at(c_, x_), BLK)
-        cp = pltpu.make_async_copy(fop_hbm.at[rows], fop.at[rows], load_sem.at[j])
-        cp.start()
-        load_fop.append(cp)
+        load_fop.append(pltpu.make_async_copy(fop_hbm.at[rows], fop.at[rows], load_sem.at[j]))
     load_obs = pltpu.make_async_copy(obs_hbm.at[:, pl.ds(mine, BLK)], obs, load_sem.at[5])
-    load_obs.start()
     load_prec = pltpu.make_async_copy(prec_hbm, prec, load_sem.at[6])
-    load_prec.start()
+    load_samp.start()
+    load_fop[0].start()
 
     barrier = pltpu.get_barrier_semaphore()
     peers = [sibling, xpart, hpart, ypeer(1), ypeer(2), ypeer(3)] + [zpeer(d) for d in range(1, 8)]
+    peers += [across(d) for d in sorted(set(RDIRECT + GDIRECT))]
     for p in peers:
         pl.semaphore_signal(barrier, inc=1, device_id=p, device_id_type=MESH)
-    pl.semaphore_wait(barrier, len(peers))
 
     def remote(src, dst, sems, i, device):
         return pltpu.make_async_remote_copy(
@@ -113,43 +115,63 @@
 
     def product(j):
         load_fop[j].wait()
+        if j < 2:
+            load_fop[j + 2].start()
+        if j == 1:
+            load_obs.start()
+            load_prec.start()
         rows = pl.ds(block_at(*order[j]), BLK)
         return jnp.dot(fop[rows, :], samp[...], preferred_element_type=F32)
 
     load_samp.wait()
+    load_fop[1].start()
     sib_send[0] = product(0)
+    pl.semaphore_wait(barrier, len(peers))
     sib0 = go(remote(sib_send.at[0], sib_recv.at[0], sib_sem, (0,), sibling))
     acc[...] = product(1)
     sib0.wait_recv()
-    xs = {}
-    for d in FAR + (0,):
-        rows = pl.ds(pl.multiple_of(((z + d) % 8) * UNIT, UNIT), UNIT)
-        x_send[d] = enc4(acc[rows, :] + sib_recv[0, rows, :])
-        xs[d] = go(remote(x_send.at[d], x_recv.at[d], x_sem, (d,), xpart))
+
+    def piece(d):
+        return pl.ds(pl.multiple_of(((z + d) % 8) * UNIT, UNIT), UNIT)
+
+    relay = tuple(d for d in FAR if d not in RDIRECT)
+    xs, zs, zxs = {}, {}, {}
+    for d in relay + RDIRECT + (0,):
+        x_send[d] = enc4(acc[piece(d), :] + sib_recv[0, piece(d), :])
+        if d in RDIRECT:
+            zxs[d] = go(remote(x_send.at[d], zx_recv.at[d], zx_sem, (d,), across(d)))
+        else:
+            xs[d] = go(remote(x_send.at[d], x_recv.at[d], x_sem, (d,), xpart))
     sib_send[1] = product(2)
     sib1 = go(remote(sib_send.at[1], sib_recv.at[1], sib_sem, (1,), sibling))
     quad[...] = product(3)
     sib1.wait_recv()
-    zs = {}
-    for d in FAR + (0,):
-        rows = pl.ds(pl.multiple_of(((z + d) % 8) * UNIT, UNIT), UNIT)
-        xs[d].wait_recv()
-        v = quad[rows, :] + sib_recv[1, rows, :] + dec4(x_recv[d])
-        if d:
-            z_send[d] = enc4(v)
-            zs[d] = go(remote(z_send.at[d], z_recv.at[d], z_sem, (d,), zpeer(d)))
-        else:
-            own[...] = v
+    quad[...] = quad[...] + sib_recv[1]
+    for d in RDIRECT + relay:
+        v = quad[piece(d), :]
+        if d in relay:
+            xs[d].wait_recv()
+            v = v + dec4(x_recv[d])
+        z_send[d] = enc4(v)
+        zs[d] = go(remote(z_send.at[d], z_recv.at[d], z_sem, (d,), zpeer(d)))
 
     load_obs.wait()
     load_prec.wait()
     obs_t[...] = obs[...].T
     prec_t[...] = jnp.broadcast_to(prec[pl.ds(mine, BLK)].reshape(1, BLK), (128, BLK)).T
 
-    pred = own[...]
-    for d in NEAR:
+    pred = quad[piece(0), :]
+    for d in RDIRECT:
         zs[d].wait_recv()
         pred = pred + dec4(z_recv[d])
+    for d in relay:
+        zs[d].wait_recv()
+        pred = pred + dec4(z_recv[d])
+    for d in RDIRECT:
+        zxs[d].wait_recv()
+        pred = pred + dec4(zx_recv[d])
+    xs[0].wait_recv()
+    pred = pred + dec4(x_recv[0])
     rows = pl.ds(pl.multiple_of(z * UNIT, UNIT), UNIT)
     p = prec_t[rows, :]
     p = jnp.concatenate([p, p], axis=1)
@@ -164,13 +186,21 @@
         zz = (z + 8 - d) % 8
         return remote(unit_at(xl, zz), unit_at(xl, zz), gx_sem, (d,), xpart)
 
-    gx = {0: go(to_x(0))}
-    gz = {}
-    for d in NEAR:
+    def direct(d):
+        return remote(unit_at(xl, z), unit_at(xl, z), gx_sem, (d,), across(d))
+
+    pass_on = tuple(d for d in FAR if d not in GDIRECT)
+    gz, gx = {}, {}
+    gx[0] = go(to_x(0))
+    for d in pass_on + GDIRECT:
         gz[d] = go(remote(unit_at(xl, z), unit_at(xl, z), gz_sem, (d,), zpeer(d)))
-    for d in NEAR:
+    for d in GDIRECT:
+        gx[d] = go(direct(d))
+    for d in pass_on:
         gz[d].wait_recv()
         gx[d] = go(to_x(d))
+    for d in GDIRECT:
+        gz[d].wait_recv()
 
     def to_sibling(k):
         b = sc_t.at[pl.ds(block_at(core, (1 - xl, xl)[k]), BLK)]
@@ -182,7 +212,7 @@
 
     g1 = go(to_sibling(1))
     turn(3)
-    for d in (0,) + NEAR:
+    for d in (0,) + GDIRECT + pass_on:
         gx[d].wait_recv()
     g0 = go(to_sibling(0))
     turn(1)
@@ -313,7 +343,7 @@
             pltpu.VMEM((2, BLK, S), F32),
             pltpu.VMEM((BLK, S), F32),
             pltpu.VMEM((BLK, S), F32),
-            pltpu.VMEM((UNIT, S), F32),
+            pltpu.VMEM((8, UNIT, S), BF16),
             pltpu.VMEM((8, UNIT, S), BF16),
             pltpu.VMEM((8, UNIT, S), BF16),
             pltpu.VMEM((8, UNIT, S), BF16),
@@ -336,6 +366,7 @@
             dma((2, 8)),
             dma((2, 8)),
             dma((2, 8)),
+            dma((2, 8)),
             dma((2, 2)),
             dma((2, XF)),
             dma((2, XF, 3)),

time: 54.5 us -> 51.1 us (0.938)
  Pallas kernels: 53.6 us -> 50.3 us
    pallas_call x1, Pallas kernels: 53.6 us -> 50.3 us  [local(): pl.pallas_call(kernel, out_shape=jax.ShapeDtypeStruct((S // 8, NB), F32),...]
where the time goes in v3:
time: 51.1 us; the launch traced here: 51 us
  Pallas kernels  50.3 us (98%)
  local copies, waits for them, and re-layouts  0.75 us (1%)
    pallas_call x1, Pallas kernels, local(): pl.pallas_call(kernel, out_shape=jax.ShapeDtypeStruct((S // 8, NB), F32),...  50.3 us

profile of v3, /device:TPU:1, one launch (start us, length us, event | category | flops | bytes accessed | tf_op | source)
XLA Modules:
  0.0 51.0 jit_solution(9457898372622425082)
XLA Ops:
  0.0 50.3 %shard_map.46 = f32[32,3072]{1,0:T(8,128)S(1)} custom-call(bf16[1536,3072]{1,0:T(8,128)(2,1)} %fop_hbm.1, bf16[3072,256]{1,0:T(8,128)(2,1)} %samp_hbm.1, f32[256,1536]{1,0:T(8,128)} %obs_hbm.1, f32[1536]{0:T(1024)} %prec_hbm.1), custom_call_target="tpu_custom_call" | custom-call | tf_op jit(solution)/shard_map/pallas_call | solution.py:330
  50.3 0.7 %copy.6 = f32[32,3072]{1,0:T(8,128)} copy(f32[32,3072]{1,0:T(8,128)S(1)} %shard_map.46) | data formatting | bytes 786432

commit v4 on v3

v4 whole, which is shorter than its diff:
```python
import jax
import jax.numpy as jnp
from jax import lax
from jax.experimental import pallas as pl
from jax.experimental.pallas import tpu as pltpu
from jax.sharding import PartitionSpec as P

MESH = pl.DeviceIdType.MESH
F32 = jnp.float32
BF16 = jnp.bfloat16

S = 256
MB = 1536
NB = 3072
UNIT = 48
BLK = 384
NC = 256
CHUNKS = NB // NC
YF = 6
XF = CHUNKS - YF
HALF = 128
EARLY = 2
TINY = 1e-36
FAR = (4, 3, 5, 2, 6, 1, 7)
DIRECT = (1, 7, 2, 6)
RELAY = (4, 3, 5)
dof = 4.0


def enc4(v):
    w = v * v
    return (v * jnp.abs(v) * w).astype(BF16)


def dec4(c):
    v = c.astype(F32)
    t = lax.rsqrt(jnp.maximum(jnp.abs(v), TINY))
    return v * (t * t * lax.rsqrt(t))


def enc2(v):
    return (v * jnp.abs(v)).astype(BF16)


def dec2(c):
    v = c.astype(F32)
    return v * lax.rsqrt(jnp.maximum(jnp.abs(v), TINY))


def student_score(error, precision):
    return (dof + 1.0) * precision * error / (dof + precision * error * error)


def kernel(
    fop_hbm, samp_hbm, obs_hbm, prec_hbm, out_ref,
    fop, samp, obs, prec, obs_t, prec_t,
    sib_send, sib_recv, acc, quad, x_send, x_recv, z_send, z_recv,
    sc_t, sc, parts, held, xx_send, xx_recv, xy_send, xy_recv, yy_send, yy_recv, yx_send, yx_recv,
    load_sem, sib_sem, x_sem, z_sem, gz_sem, gx_sem, gs_sem, xx_sem, xy_sem, yy_sem, yx_sem,
):
    row = lax.axis_index("row")
    col = lax.axis_index("col")
    xh, y = row // 4, row % 4
    xl, z, core = col // 16, (col // 2) % 8, col % 2

    def at_col(x_, z_, c_):
        return (row, x_ * 16 + z_ * 2 + c_)

    sibling = at_col(xl, z, 1 - core)
    xpart = at_col(1 - xl, z, core)
    hpart = ((1 - xh) * 4 + y, col)

    def zpeer(d):
        return at_col(xl, (z + d) % 8, core)

    def across(d):
        return at_col(1 - xl, (z + d) % 8, core)

    def ypeer(d):
        return (xh * 4 + (y + d) % 4, col)

    def block_at(c_, x_):
        return pl.multiple_of((c_ * 2 + x_) * BLK, BLK)

    order = ((1 - core, 1 - xl), (core, 1 - xl), (1 - core, xl), (core, xl))
    mine = block_at(core, xl)

    load_samp = pltpu.make_async_copy(samp_hbm, samp, load_sem.at[4])
    load_fop = []
    for j, (c_, x_) in enumerate(order):
        rows = pl.ds(block_at(c_, x_), BLK)
        load_fop.append(pltpu.make_async_copy(fop_hbm.at[rows], fop.at[rows], load_sem.at[j]))
    load_obs = pltpu.make_async_copy(obs_hbm.at[:, pl.ds(mine, BLK)], obs, load_sem.at[5])
    load_prec = pltpu.make_async_copy(prec_hbm, prec, load_sem.at[6])
    load_samp.start()
    load_fop[0].start()

    barrier = pltpu.get_barrier_semaphore()
    peers = [sibling, xpart, hpart, ypeer(1), ypeer(2), ypeer(3)] + [zpeer(d) for d in range(1, 8)]
    peers += [across(d) for d in DIRECT]
    for p in peers:
        pl.semaphore_signal(barrier, inc=1, device_id=p, device_id_type=MESH)

    def remote(src, dst, sems, i, device):
        return pltpu.make_async_remote_copy(
            src_ref=src, dst_ref=dst, send_sem=sems.at[(0,) + i], recv_sem=sems.at[(1,) + i],
            device_id=device, device_id_type=MESH,
        )

    sends = []

    def go(cp):
        cp.start()
        sends.append(cp)
        return cp

    def product(j):
        load_fop[j].wait()
        if j < 2:
            load_fop[j + 2].start()
        if j == 1:
            load_obs.start()
            load_prec.start()
        rows = pl.ds(block_at(*order[j]), BLK)
        return jnp.dot(fop[rows, :], samp[...], preferred_element_type=F32)

    load_samp.wait()
    load_fop[1].start()
    sib_send[0] = product(0)
    pl.semaphore_wait(barrier, len(peers))
    sib0 = go(remote(sib_send.at[0], sib_recv.at[0], sib_sem, (0,), sibling))
    acc[...] = product(1)
    sib0.wait_recv()

    def piece(d):
        return pl.ds(pl.multiple_of(((z + d) % 8) * UNIT, UNIT), UNIT)

    lanes = [pl.ds(pl.multiple_of(x_ * HALF, HALF), HALF) for x_ in (1 - xh, xh)]
    xs, zs, gz, gx = {}, {}, {}, {}

    def send_x(k):
        for d in FAR + (0,):
            x_send[k, d] = enc4(acc[piece(d), lanes[k]] + sib_recv[0, piece(d), lanes[k]])
            xs[k, d] = go(remote(x_send.at[k, d], x_recv.at[k, d], x_sem, (k, d), xpart))

    def send_z(k):
        for d in FAR:
            xs[k, d].wait_recv()
            z_send[k, d] = enc4(quad[piece(d), lanes[k]] + dec4(x_recv[k, d]))
            zs[k, d] = go(remote(z_send.at[k, d], z_recv.at[k, d], z_sem, (k, d), zpeer(d)))

    def unit_at(k, x_, z_):
        return sc_t.at[k, pl.ds(pl.multiple_of((core * 2 + x_) * BLK + z_ * UNIT, 16), UNIT)]

    def score(k):
        pred = quad[piece(0), lanes[k]]
        xs[k, 0].wait_recv()
        pred = pred + dec4(x_recv[k, 0])
        for d in FAR:
            zs[k, d].wait_recv()
            pred = pred + dec4(z_recv[k, d])
        error = obs_t[piece(0), lanes[k]] - pred
        unit_at(k, xl, z)[...] = student_score(error, prec_t[piece(0), :]).astype(BF16)

    def own_to(k, sem, d, device):
        return go(remote(unit_at(k, xl, z), unit_at(k, xl, z), sem, (k, d), device))

    def to_x(k, d):
        u = unit_at(k, xl, (z + 8 - d) % 8)
        return go(remote(u, u, gx_sem, (k, d), xpart))

    def gather(k):
        gx[k, 0] = to_x(k, 0)
        for d in RELAY + DIRECT:
            gz[k, d] = own_to(k, gz_sem, d, zpeer(d))
        for d in DIRECT:
            gx[k, d] = own_to(k, gx_sem, d, across(d))

    def relay(k):
        for d in RELAY:
            gz[k, d].wait_recv()
            gx[k, d] = to_x(k, d)
        for d in DIRECT:
            gz[k, d].wait_recv()

    def to_sibling(k, x_, i):
        b = sc_t.at[k, pl.ds(block_at(core, x_), BLK)]
        return go(remote(b, b, gs_sem, (k, i), sibling))

    def turn(k, c_, x_):
        b = pl.ds(block_at(c_, x_), BLK)
        sc[k, :, b] = sc_t[k, b, :].T

    def share_own(k):
        cp = to_sibling(k, xl, 0)
        turn(k, core, xl)
        return cp

    def share_other(k):
        for d in (0,) + DIRECT + RELAY:
            gx[k, d].wait_recv()
        cp = to_sibling(k, 1 - xl, 1)
        turn(k, core, 1 - xl)
        return cp

    def complete(k, first, second):
        first.wait_recv()
        turn(k, 1 - core, xl)
        second.wait_recv()
        turn(k, 1 - core, 1 - xl)

    send_x(0)
    send_x(1)
    sib_send[1] = product(2)
    sib1 = go(remote(sib_send.at[1], sib_recv.at[1], sib_sem, (1,), sibling))
    quad[...] = product(3)
    sib1.wait_recv()
    quad[...] = quad[...] + sib_recv[1]
    send_z(0)
    load_obs.wait()
    load_prec.wait()
    obs_t[...] = obs[...].T
    prec_t[...] = jnp.broadcast_to(prec[pl.ds(mine, BLK)].reshape(1, BLK), (HALF, BLK)).T
    send_z(1)
    score(0)
    gather(0)
    score(1)
    gather(1)
    relay(0)
    first0 = share_own(0)
    relay(1)
    second0 = share_other(0)
    complete(0, first0, second0)

    def columns(c):
        return pl.ds(pl.multiple_of(c * NC, NC), NC)

    def dest(y_):
        return pl.ds(pl.multiple_of(y_ * 32, 32), 32)

    def xx(i):
        return remote(xx_send.at[i], xx_recv.at[i], xx_sem, (i,), hpart)

    def xy(i, d):
        return remote(xy_send.at[i, d - 1], xy_recv.at[i, d - 1], xy_sem, (i, d - 1), ypeer(d))

    def yy(k, j, d):
        return remote(yy_send.at[k, j, d - 1], yy_recv.at[k, j, d - 1], yy_sem, (k, j, d - 1), ypeer(d))

    def yx(j):
        return remote(yx_send.at[j], yx_recv.at[j], yx_sem, (j,), hpart)

    def adjoint(k, c):
        return jnp.dot(sc[k], fop[:, columns(c)], preferred_element_type=F32)

    def x_other(i, c):
        xx_send[i] = enc2(adjoint(0, c))
        xx(i).start()

    def x_mine(i, c):
        parts[1, c] = adjoint(1, c)

    def y_part(k, j, c):
        parts[k, c] = adjoint(k, c)
        for d in (2, 1, 3):
            yy_send[k, j, d - 1] = enc2(parts[k, c, dest((y + d) % 4), :])
            yy(k, j, d).start()

    def y_other(j, c):
        y_part(0, j, c)

    def y_mine(j, c):
        y_part(1, j, c)

    def x_then_y(i, c):
        xx(i).wait_recv()
        for d in (2, 1, 3, 0):
            at = dest((y + d) % 4)
            v = parts[1, c, at, :] + dec2(xx_recv[i, at, :])
            if d:
                xy_send[i, d - 1] = enc2(v)
                xy(i, d).start()
            else:
                held[c] = v

    def y_total(k, j, c):
        v = parts[k, c, dest(y), :]
        for d in (1, 3, 2):
            yy(k, j, d).wait_recv()
            v = v + dec2(yy_recv[k, j, d - 1])
        return v

    def y_then_x(j, c):
        yx_send[j] = enc2(y_total(0, j, c))
        yx(j).start()

    def end_x_first(i, c):
        v = held[c]
        for d in (1, 3, 2):
            xy(i, d).wait_recv()
            v = v + dec2(xy_recv[i, d - 1])
        out_ref[:, columns(c)] = v

    def end_y_first(j, c):
        v = y_total(1, j, c)
        yx(j).wait_recv()
        out_ref[:, columns(c)] = v + dec2(yx_recv[j])

    def drain_x(i, c):
        xx(i).wait_send()
        for d in (1, 2, 3):
            xy(i, d).wait_send()

    def drain_y(j, c):
        yx(j).wait_send()
        for k in range(2):
            for d in (1, 2, 3):
                yy(k, j, d).wait_send()

    pairs = min(XF, YF)

    def sweep(on_x, on_y, lo=0, hi=CHUNKS):
        def both(t, carry):
            on_x(t, 2 * t)
            on_y(t, 2 * t + 1)
            return carry

        def rest(t, carry):
            (on_y if YF > XF else on_x)(t, t + pairs)
            return carry

        lax.fori_loop(lo, min(hi, pairs), both, 0)
        if hi > pairs and XF != YF:
            lax.fori_loop(max(lo, pairs), max(XF, YF), rest, 0)

    sweep(x_other, y_other, 0, EARLY)
    first1 = share_own(1)
    second1 = share_other(1)
    sweep(x_other, y_other, EARLY)
    complete(1, first1, second1)
    sweep(x_mine, y_mine)
    sweep(x_then_y, y_then_x)
    sweep(end_x_first, end_y_first)
    for cp in sends:
        cp.wait_send()
    sweep(drain_x, drain_y)


def local(forward_op, samples, observed, precision):
    dma = pltpu.SemaphoreType.DMA
    return pl.pallas_call(
        kernel,
        out_shape=jax.ShapeDtypeStruct((S // 8, NB), F32),
        in_specs=[pl.BlockSpec(memory_space=pltpu.HBM)] * 4,
        out_specs=pl.BlockSpec(memory_space=pltpu.VMEM),
        scratch_shapes=[
            pltpu.VMEM((MB, NB), BF16),
            pltpu.VMEM((NB, S), BF16),
            pltpu.VMEM((S, BLK), F32),
            pltpu.VMEM((MB,), F32),
            pltpu.VMEM((BLK, S), F32),
            pltpu.VMEM((BLK, 128), F32),
            pltpu.VMEM((2, BLK, S), F32),
            pltpu.VMEM((2, BLK, S), F32),
            pltpu.VMEM((BLK, S), F32),
            pltpu.VMEM((BLK, S), F32),
            pltpu.VMEM((2, 8, UNIT, HALF), BF16),
            pltpu.VMEM((2, 8, UNIT, HALF), BF16),
            pltpu.VMEM((2, 8, UNIT, HALF), BF16),
            pltpu.VMEM((2, 8, UNIT, HALF), BF16),
            pltpu.VMEM((2, MB, HALF), BF16),
            pltpu.VMEM((2, HALF, MB), BF16),
            pltpu.VMEM((2, CHUNKS, HALF, NC), F32),
            pltpu.VMEM((CHUNKS, 32, NC), F32),
            pltpu.VMEM((XF, HALF, NC), BF16),
            pltpu.VMEM((XF, HALF, NC), BF16),
            pltpu.VMEM((XF, 3, 32, NC), BF16),
            pltpu.VMEM((XF, 3, 32, NC), BF16),
            pltpu.VMEM((2, YF, 3, 32, NC), BF16),
            pltpu.VMEM((2, YF, 3, 32, NC), BF16),
            pltpu.VMEM((YF, 32, NC), BF16),
            pltpu.VMEM((YF, 32, NC), BF16),
            dma((7,)),
            dma((2, 2)),
            dma((2, 2, 8)),
            dma((2, 2, 8)),
            dma((2, 2, 8)),
            dma((2, 2, 8)),
            dma((2, 2, 2)),
            dma((2, XF)),
            dma((2, XF, 3)),
            dma((2, 2, YF, 3)),
            dma((2, YF)),
        ],
        compiler_params=pltpu.CompilerParams(
            collective_id=0, has_side_effects=True, vmem_limit_bytes=48 * 1024 * 1024
        ),
    )(*[pltpu.with_memory_space_constraint(a, pltpu.HBM) for a in (forward_op, samples, observed, precision)])


def solution(mesh):
    return jax.shard_map(
        local,
        mesh=mesh,
        in_specs=(P("row", "col"), P("col", None), P(None, "row"), P("row")),
        out_specs=P("row", "col"),
        check_vma=False,
    )
```

time: 51.1 us -> 49.3 us (0.965)
  Pallas kernels: 50.3 us -> 48.5 us
    pallas_call x1, Pallas kernels: 50.3 us -> 48.5 us  [local(): pl.pallas_call(kernel, out_shape=jax.ShapeDtypeStruct((S // 8, NB), F32),...]
where the time goes in v4:
time: 49.3 us; the launch traced here: 49.2 us
  Pallas kernels  48.5 us (98%)
  local copies, waits for them, and re-layouts  0.75 us (2%)
    pallas_call x1, Pallas kernels, local(): pl.pallas_call(kernel, out_shape=jax.ShapeDtypeStruct((S // 8, NB), F32),...  48.5 us

profile of v4, /device:TPU:1, one launch (start us, length us, event | category | flops | bytes accessed | tf_op | source)
XLA Modules:
  0.0 49.2 jit_solution(3664505867161553951)
XLA Ops:
  0.0 48.5 %shard_map.46 = f32[32,3072]{1,0:T(8,128)S(1)} custom-call(bf16[1536,3072]{1,0:T(8,128)(2,1)} %fop_hbm.1, bf16[3072,256]{1,0:T(8,128)(2,1)} %samp_hbm.1, f32[256,1536]{1,0:T(8,128)} %obs_hbm.1, f32[1536]{0:T(1024)} %prec_hbm.1), custom_call_target="tpu_custom_call" | custom-call | tf_op jit(solution)/shard_map/pallas_call | solution.py:351
  48.5 0.7 %copy.6 = f32[32,3072]{1,0:T(8,128)} copy(f32[32,3072]{1,0:T(8,128)S(1)} %shard_map.46) | data formatting | bytes 786432

commit v5 on v4

--- a/solution.py
+++ b/solution.py
@@ -14,9 +14,9 @@
 NB = 3072
 UNIT = 48
 BLK = 384
-NC = 256
+NC = 512
 CHUNKS = NB // NC
-YF = 6
+YF = 3
 XF = CHUNKS - YF
 HALF = 128
 EARLY = 2
@@ -306,16 +306,20 @@
         yx(j).wait_recv()
         out_ref[:, columns(c)] = v + dec2(yx_recv[j])
 
+    def sent_x(i, c):
+        xx(i).wait_send()
+
     def drain_x(i, c):
-        xx(i).wait_send()
         for d in (1, 2, 3):
             xy(i, d).wait_send()
 
-    def drain_y(j, c):
-        yx(j).wait_send()
+    def sent_y(j, c):
         for k in range(2):
             for d in (1, 2, 3):
                 yy(k, j, d).wait_send()
+
+    def drain_y(j, c):
+        yx(j).wait_send()
 
     pairs = min(XF, YF)
 
@@ -339,10 +343,11 @@
     sweep(x_other, y_other, EARLY)
     complete(1, first1, second1)
     sweep(x_mine, y_mine)
-    sweep(x_then_y, y_then_x)
-    sweep(end_x_first, end_y_first)
     for cp in sends:
         cp.wait_send()
+    sweep(x_then_y, y_then_x)
+    sweep(sent_x, sent_y)
+    sweep(end_x_first, end_y_first)
     sweep(drain_x, drain_y)
 
 

time: 49.3 us -> 49.1 us (level)
  no operation moved by 1% of the time
where the time goes in v5:
time: 49.1 us; the launch traced here: 49 us
  Pallas kernels  48.2 us (98%)
  local copies, waits for them, and re-layouts  0.75 us (2%)
    pallas_call x1, Pallas kernels, local(): pl.pallas_call(kernel, out_shape=jax.ShapeDtypeStruct((S // 8, NB), F32),...  48.2 us

profile of v5, /device:TPU:1, one launch (start us, length us, event | category | flops | bytes accessed | tf_op | source)
XLA Modules:
  0.0 49.0 jit_solution(17244374272453018048)
XLA Ops:
  0.0 48.2 %shard_map.46 = f32[32,3072]{1,0:T(8,128)S(1)} custom-call(bf16[1536,3072]{1,0:T(8,128)(2,1)} %fop_hbm.1, bf16[3072,256]{1,0:T(8,128)(2,1)} %samp_hbm.1, f32[256,1536]{1,0:T(8,128)} %obs_hbm.1, f32[1536]{0:T(1024)} %prec_hbm.1), custom_call_target="tpu_custom_call" | custom-call | tf_op jit(solution)/shard_map/pallas_call | solution.py:356
  48.2 0.7 %copy.6 = f32[32,3072]{1,0:T(8,128)} copy(f32[32,3072]{1,0:T(8,128)S(1)} %shard_map.46) | data formatting | bytes 786432
